TPU v7x, 512 devices: a whole 4x8x8 slice. The times are simulated.
512 devices in a mesh: tm: 32 (over y, x), chan: 16 (over z, core).
Axes of the slice: x: 4, y: 8, z: 8, core: 2. Of those that a mesh axis runs over, the one named last changes fastest.
Arguments:
- record: bfloat16 [32768, 10240], P('tm', 'chan'), may hold values from -6 to 6
- fir_taps: bfloat16 [64], replicated, may hold values from -0.75 to 0.75
- gauge_lag: int32 [10240], P('chan'), may hold values from 1 to 16
- projector: bfloat16 [32768, 128], P('tm'), may hold values from -0.1875 to 0.1875
- compress: float32 [256, 128], replicated, may hold values from -0.5 to 0.5
Outputs:
- sketch: float32 [128, 10240], P('tm', 'chan')
Inputs may be any that keep to these rules, and one draw needn't show every extreme that they name: `gauge_lag`: some channel has lag 16.
All inputs are finite; a program needn't handle non-finite values.
Results may differ from a plain program's by a relative error of at most 0.0028.
Values may be sent and summed in bfloat16 or wider, within the bound.
A program may use at most 64 MiB of HBM per device.

v0:
```python
import jax
import jax.numpy as jnp
from jax import lax
from jax.sharding import PartitionSpec as P

TAPS = 64
GAUGE_MAX = 16
K_ITERS = 8


def from_behind(value, axis, steps):
    count = lax.axis_size(axis)
    first, last = (max(0, -steps), min(count, count - steps))
    return lax.ppermute(value, axis, [(source, source + steps) for source in range(first, last)])


def from_partner(value, axis, bit):
    mask = 2**bit
    pairs = [(source, source ^ mask) for source in range(lax.axis_size(axis))]
    return lax.ppermute(value, axis, pairs)


def toeplitz_block(fir_taps, out_count):
    row_ids = jnp.arange(out_count, dtype=jnp.int32)[:, None]
    col_ids = jnp.arange(out_count + TAPS - 1, dtype=jnp.int32)[None, :]
    offset = row_ids + TAPS - 1 - col_ids
    tap_ids = jnp.arange(TAPS, dtype=jnp.int32)
    onehot = (offset[:, :, None] == tap_ids[None, None, :]).astype(jnp.float32)
    return jnp.sum(onehot * fir_taps.astype(jnp.float32)[None, None, :], axis=2).astype(
        jnp.bfloat16
    )


def filter_mix(gram, compress):
    width = gram.shape[0]
    eye = jnp.eye(width, dtype=jnp.float32)
    mean_level = jnp.trace(gram) / width
    shifted = gram - mean_level * eye
    signed = shifted / jnp.sqrt(jnp.sum(shifted * shifted) + 1e-06)
    for step_index in range(K_ITERS):
        square = jnp.dot(
            signed, signed, precision=lax.Precision.HIGHEST, preferred_element_type=jnp.float32
        )
        signed = jnp.dot(
            signed,
            1.5 * eye - 0.5 * square,
            precision=lax.Precision.HIGHEST,
            preferred_element_type=jnp.float32,
        )
    filter_mat = 0.5 * (eye + signed)
    return jnp.dot(
        compress.T, filter_mat, precision=lax.Precision.HIGHEST, preferred_element_type=jnp.float32
    )


def inner_rows(first_mat, second_mat):
    return jnp.dot(
        first_mat, second_mat.T, precision=lax.Precision.HIGHEST, preferred_element_type=jnp.float32
    )


def on_device(record, fir_taps, gauge_lag, projector, compress):
    sample_rows = record.shape[0]
    column_count = record.shape[1]
    halo_rows = TAPS - 1 + GAUGE_MAX
    tail_rows = record[sample_rows - halo_rows :]
    before = from_behind(tail_rows, "tm", 1)
    extended = jnp.concatenate([before, record], 0)
    lead_matrix = toeplitz_block(fir_taps, GAUGE_MAX)
    lead_part = jnp.dot(
        lead_matrix, extended[: GAUGE_MAX + TAPS - 1], preferred_element_type=jnp.float32
    )
    block_rows = min(128, sample_rows)
    main_matrix = toeplitz_block(fir_taps, block_rows)

    def filter_block(block_index):
        segment = lax.dynamic_slice_in_dim(
            extended, GAUGE_MAX + block_index * block_rows, block_rows + TAPS - 1, 0
        )
        return jnp.dot(main_matrix, segment, preferred_element_type=jnp.float32)

    main_part = lax.map(filter_block, jnp.arange(sample_rows // block_rows, dtype=jnp.int32))
    filtered = jnp.concatenate([lead_part, main_part.reshape(sample_rows, column_count)], 0)
    current = filtered[GAUGE_MAX:]
    lagged = jnp.zeros((sample_rows, column_count), jnp.float32)
    for lag_step in range(1, GAUGE_MAX + 1):
        chosen = (gauge_lag == lag_step).astype(jnp.float32)[None, :]
        lagged = (
            lagged + chosen * filtered[GAUGE_MAX - lag_step : GAUGE_MAX - lag_step + sample_rows]
        )
    strain = (current - lagged).astype(jnp.bfloat16)
    sketch = lax.dot_general(
        projector, strain, (((0,), (0,)), ((), ())), preferred_element_type=jnp.float32
    )
    depth_count = lax.axis_size("tm").bit_length() - 1
    position = lax.axis_index("tm")
    for depth_level in range(depth_count):
        is_lower = position // 2**depth_level % 2 == 0
        partner = from_partner(sketch, "tm", depth_level)
        stacked = jnp.where(
            is_lower, jnp.concatenate([sketch, partner], 0), jnp.concatenate([partner, sketch], 0)
        )
        gram = lax.psum(inner_rows(stacked, stacked), "chan")
        mixing = filter_mix(gram, compress)
        sketch = jnp.dot(
            mixing, stacked, precision=lax.Precision.HIGHEST, preferred_element_type=jnp.float32
        )
    share_rows = sketch.shape[0] // lax.axis_size("tm")
    return lax.dynamic_slice_in_dim(sketch, position * share_rows, share_rows, 0)


def solution(mesh):
    return jax.shard_map(
        on_device,
        mesh=mesh,
        in_specs=(P("tm", "chan"), P(), P("chan"), P("tm", None), P()),
        out_specs=P("tm", "chan"),
        check_vma=False,
    )
```

profile of v0, /device:TPU:1, one launch (start us, length us, event | category | flops | bytes accessed | tf_op | source)
XLA Modules:
  0.0 803.2 jit_solution(263706194352711852)
XLA Ops:
  7.5 3.9 collective-permute-start
  12.2 2.0 select_reduce_fusion
  15.2 1.6 pad_maximum_fusion.1
  16.9 19.6 %while.12 = (s32[]{:T(128)}, f32[8,128,640]{2,1,0:T(8,128)}, s32[8]{0:T(128)S(1)}, bf16[1103,640]{1,0:T(8,128)(2,1)S(1)}, bf16[128,191]{1,0:T(8,128)(2,1)S(1)}, ...) while((s32[]{:T(128)}, f32[8,128,640]{2,1,0:T(8,128)}, s32[8]{0:T(128)S(1)}, ...), condition=%wide.region_2.3_spmd, body=%wide.region_1.0_spmd.sunk | while | flops 31293448 | bytes 1949883 | solution.py:82
  36.6 24.8 %fusion.52 = f32[128,640]{1,0:T(8,128)S(1)} fusion(bf16[1024,128]{1,0:T(8,128)(2,1)S(1)} %copy-done, f32[1024,640]{1,0:T(8,128)} %bitcast.181, f32[16,640]{1,0:T(8,128)S(1)} %fusion.158, f32[640]{0:T(1024)S(1)} %get-tuple-element.100, f32[640]{0:T(1024)S(1)} %get-tuple-element.101, f32[640]{0:T(1024)S(1)} %get-tuple-element.87, ...), kind=kOutput, calls=%fused_computation.121 | convolution fusion | flops 199884800 | bytes 3293184 | tf_op jit(solution)/shard_map/dot_general | solution.py:92
  61.4 3.1 collective-permute-start.1
  64.6 4.7 collective-permute-done.1
  71.4 123.7 %all-reduce.6.cloned.1.call-done = f32[256,256]{1,0:T(8,128)} async-done(((f32[256,256]{1,0:T(8,128)}), f32[256,256]{1,0:T(8,128)}) %all-reduce.6.cloned.1.call-update) | async-done | bytes 262160 | tf_op jit(solution)/shard_map/psum | solution.py:103
  197.4 1.6 multiply_reduce_fusion.4
  209.1 4.6 collective-permute-start.2
  213.8 7.4 collective-permute-done.2
  223.0 115.3 %all-reduce.8.cloned.1.call-done = f32[256,256]{1,0:T(8,128)} async-done(((f32[256,256]{1,0:T(8,128)}), f32[256,256]{1,0:T(8,128)}) %all-reduce.8.cloned.1.call-update) | async-done | bytes 262160 | tf_op jit(solution)/shard_map/psum | solution.py:103
  340.5 1.6 multiply_reduce_fusion.3
  352.3 3.1 collective-permute-start.3
  355.4 7.4 collective-permute-done.3
  364.6 115.3 %all-reduce.10.cloned.1.call-done = f32[256,256]{1,0:T(8,128)} async-done(((f32[256,256]{1,0:T(8,128)}), f32[256,256]{1,0:T(8,128)}) %all-reduce.10.cloned.1.call-update) | async-done | bytes 262160 | tf_op jit(solution)/shard_map/psum | solution.py:103
  482.2 1.6 multiply_reduce_fusion.2
  493.9 4.0 collective-permute-start.4
  498.0 14.5 %collective-permute-done.4 = f32[128,640]{1,0:T(8,128)S(1)} collective-permute-done((f32[128,640]{1,0:T(8,128)S(1)}, f32[128,640]{1,0:T(8,128)S(1)}, u32[]{:S(2)}, u32[]{:S(2)}) %collective-permute-start.4) | collective-permute-done | bytes 327712 | tf_op jit(solution)/shard_map/ppermute | solution.py:20
  514.3 115.4 %all-reduce.12.cloned.1.call-done = f32[256,256]{1,0:T(8,128)} async-done(((f32[256,256]{1,0:T(8,128)}), f32[256,256]{1,0:T(8,128)}) %all-reduce.12.cloned.1.call-update) | async-done | bytes 262160 | tf_op jit(solution)/shard_map/psum | solution.py:103
  631.9 1.6 multiply_reduce_fusion.1
  643.7 7.4 collective-permute-start.5
  651.1 8.9 %collective-permute-done.5 = f32[128,640]{1,0:T(8,128)S(1)} collective-permute-done((f32[128,640]{1,0:T(8,128)S(1)}, f32[128,640]{1,0:T(8,128)S(1)}, u32[]{:S(2)}, u32[]{:S(2)}) %collective-permute-start.5) | collective-permute-done | bytes 327712 | tf_op jit(solution)/shard_map/ppermute | solution.py:20
  661.6 120.0 %all-reduce.14.cloned.1.call-done = f32[256,256]{1,0:T(8,128)} async-done(((f32[256,256]{1,0:T(8,128)}), f32[256,256]{1,0:T(8,128)}) %all-reduce.14.cloned.1.call-update) | async-done | bytes 262160 | tf_op jit(solution)/shard_map/psum | solution.py:103
  (161 shorter events, 83.0 us)
Async XLA Ops:
  6.5 30.1 %copy-start = (bf16[1024,128]{1,0:T(8,128)(2,1)S(1)}, bf16[1024,128]{1,0:T(8,128)(2,1)}, u32[]{:S(2)}) copy-start(bf16[1024,128]{1,0:T(8,128)(2,1)} %param.10) | copy-start | bytes 786436
  6.5 188.6 %all-reduce.6.cloned.1.call-start = ((), (), s32[]{:S(2)}) async-start(), calls=%async_computation | async-start | bytes 524288 | tf_op jit(solution)/shard_map/psum | solution.py:103
  7.5 7.7 collective-permute-start
  61.4 7.8 collective-permute-start.1
  70.8 267.5 %all-reduce.8.cloned.1.call-start = ((), (), s32[]{:S(2)}) async-start(), calls=%async_computation.1 | async-start | bytes 524288 | tf_op jit(solution)/shard_map/psum | solution.py:103
  205.2 2.7 copy-start.1
  209.1 12.1 %collective-permute-start.2 = (f32[128,640]{1,0:T(8,128)S(1)}, f32[128,640]{1,0:T(8,128)S(1)}, u32[]{:S(2)}, u32[]{:S(2)}) collective-permute-start(f32[128,640]{1,0:T(8,128)S(1)} %fusion.68), channel_id=1, source_target_pairs={{0,32},{16,48},{32,0},{48,16},{64,96},{80,112},{96,64},{112,80},{1... | collective-permute-start | bytes 983048 | tf_op jit(solution)/shard_map/ppermute | solution.py:20
  222.7 257.2 %all-reduce.10.cloned.1.call-start = ((), (), s32[]{:S(2)}) async-start(), calls=%async_computation.2 | async-start | bytes 524288 | tf_op jit(solution)/shard_map/psum | solution.py:103
  352.3 10.5 %collective-permute-start.3 = (f32[128,640]{1,0:T(8,128)S(1)}, f32[128,640]{1,0:T(8,128)S(1)}, u32[]{:S(2)}, u32[]{:S(2)}) collective-permute-start(f32[128,640]{1,0:T(8,128)S(1)} %fusion.66), channel_id=1, source_target_pairs={{0,64},{16,80},{32,96},{48,112},{64,0},{80,16},{96,32},{112,48},{1... | collective-permute-start | bytes 983048 | tf_op jit(solution)/shard_map/ppermute | solution.py:20
  364.4 265.3 %all-reduce.12.cloned.1.call-start = ((), (), s32[]{:S(2)}) async-start(), calls=%async_computation.3 | async-start | bytes 524288 | tf_op jit(solution)/shard_map/psum | solution.py:103
  493.9 18.5 %collective-permute-start.4 = (f32[128,640]{1,0:T(8,128)S(1)}, f32[128,640]{1,0:T(8,128)S(1)}, u32[]{:S(2)}, u32[]{:S(2)}) collective-permute-start(f32[128,640]{1,0:T(8,128)S(1)} %fusion.64), channel_id=1, source_target_pairs={{0,128},{16,144},{32,160},{48,176},{64,192},{80,208},{96,224},{112... | collective-permute-start | bytes 983048 | tf_op jit(solution)/shard_map/ppermute | solution.py:20
  514.0 267.6 %all-reduce.14.cloned.1.call-start = ((), (), s32[]{:S(2)}) async-start(), calls=%async_computation.4 | async-start | bytes 524288 | tf_op jit(solution)/shard_map/psum | solution.py:103
  643.7 16.3 %collective-permute-start.5 = (f32[128,640]{1,0:T(8,128)S(1)}, f32[128,640]{1,0:T(8,128)S(1)}, u32[]{:S(2)}, u32[]{:S(2)}) collective-permute-start(f32[128,640]{1,0:T(8,128)S(1)} %fusion.62), channel_id=1, source_target_pairs={{0,256},{16,272},{32,288},{48,304},{64,320},{80,336},{96,352},{112... | collective-permute-start | bytes 983048 | tf_op jit(solution)/shard_map/ppermute | solution.py:20
Sparse Core Ops, SparseCore 0:
  70.9 124.1 all-reduce.5
  222.9 115.3 all-reduce.7
  364.5 115.3 all-reduce.9
  514.1 115.5 all-reduce.11
  661.7 119.8 all-reduce.13
where the time goes:
time: 809 us; the launch traced here: 803 us
  waiting for transfers between devices  633 us (78%)
  matrix products  81.5 us (10%)
  starting transfers between devices  27.5 us (3%)
  other arithmetic  21.4 us (3%)
  between operations  21.3 us (3%)
  local copies, waits for them, and re-layouts  13.8 us (2%)
    psum x5, waiting for transfers between devices, on_device(): gram = lax.psum(inner_rows(stacked, stacked), 'chan')  590 us
    ppermute x5, waiting for transfers between devices, from_partner(): return lax.ppermute(value, axis, pairs)  42.9 us
    dot_general x1, matrix products, on_device(): lax.dot_general(projector, strain, (((0,), (0,)), ((), ())), preferred_el...  24.8 us
    ppermute x5, starting transfers between devices, from_partner(): return lax.ppermute(value, axis, pairs)  22.3 us
    dot_general x40, matrix products, filter_mix(): jnp.dot(signed, signed, precision=lax.Precision.HIGHEST, preferred_elemen...  20.5 us
    dot_general x40, matrix products, filter_mix(): jnp.dot(signed, 1.5 * eye - 0.5 * square, precision=lax.Precision.HIGHEST...  20 us
  transfers between devices with their start and end apart: 11, of which 10 were waited for; matrix products, arithmetic and copies ran while one was open for 0% of the time, Pallas kernels for 0%

commit v1 on v0

v1 whole, which is shorter than its diff:
```python
import functools

import jax
import jax.numpy as jnp
from jax import lax
from jax.experimental import pallas as pl
from jax.experimental.pallas import tpu as pltpu
from jax.sharding import PartitionSpec as P

TAPS = 64
GAUGE_MAX = 16
K_ITERS = 8
HALO = 80
RANK = 128
BLOCK = 128
MESH = pl.DeviceIdType.MESH
F32 = jnp.float32
BF16 = jnp.bfloat16


def split(value):
    high = value.astype(BF16)
    return high, (value - high.astype(F32)).astype(BF16)


def dot(first, second, contract=((1,), (0,))):
    return lax.dot_general(first, second, (contract, ((), ())), preferred_element_type=F32)


def dot3(first, second, contract=((1,), (0,))):
    fh, fl = first
    sh, sl = second
    return dot(fh, sh, contract) + (dot(fh, sl, contract) + dot(fl, sh, contract))


NT = ((1,), (1,))
TN = ((0,), (0,))


def kernel(n_tm, n_chan, levels, record, base_ref, lag_ref, proj_ref, comp_ref, out_ref,
           ext, filtered, strain, stk, stk_hi, stk_lo, gram, diag, comp_t, part, scat, gath,
           z_ref, a_ref, b_ref, local_sem, halo_sem, ex_sem, dg_sem, rs_send, rs_recv, ag_send, ag_recv):
    tm = lax.axis_index("tm")
    me = lax.axis_index("chan")
    n_rows, n_cols = record.shape
    slice_rows = RANK // n_chan
    n_blocks = n_rows // BLOCK
    n_tiles = n_cols // 128

    load = pltpu.make_async_copy(record, ext.at[pl.ds(HALO, n_rows)], local_sem)
    load.start()

    nxt = lax.rem(tm + 1, n_tm)
    prv = lax.rem(tm + n_tm - 1, n_tm)
    partners = []
    for level in range(levels):
        bit = 2**level
        partners.append(tm + bit * (1 - 2 * lax.rem(tm // bit, 2)))
    offsets = sorted(range(1, n_chan), key=lambda o: -min(o, n_chan - o))

    barrier = pltpu.get_barrier_semaphore()
    for who in [nxt, prv] + partners:
        pl.semaphore_signal(barrier, inc=1, device_id={"tm": who}, device_id_type=MESH)
    for o in offsets:
        pl.semaphore_signal(barrier, inc=1, device_id={"chan": lax.rem(me + o, n_chan)}, device_id_type=MESH)
    pl.semaphore_wait(barrier, 2 + levels + n_chan - 1)

    halo = pltpu.make_async_remote_copy(
        src_ref=record.at[pl.ds(n_rows - HALO, HALO)], dst_ref=ext.at[pl.ds(0, HALO)],
        send_sem=halo_sem.at[0], recv_sem=halo_sem.at[1], device_id={"tm": nxt}, device_id_type=MESH)
    halo.start()

    toeplitz = pltpu.roll(jnp.broadcast_to(base_ref[...], (BLOCK, 256)), 0, 1, stride=1, stride_axis=0)
    toeplitz = toeplitz[:, :BLOCK + TAPS].astype(BF16)
    comp = comp_ref[...].T
    comp_t[0] = comp
    comp_t[1, :, 0:RANK] = comp[:, RANK:]
    comp_t[1, :, RANK:] = comp[:, :RANK]
    load.wait()

    def fir(block):
        start = pl.multiple_of(block * BLOCK, BLOCK)
        window = ext[pl.ds(start + GAUGE_MAX, BLOCK + TAPS)]
        filtered[pl.ds(start + GAUGE_MAX, BLOCK)] = dot(toeplitz, window)

    @pl.loop(1, n_blocks)
    def _(block):
        fir(block)

    halo.wait()
    ext[pl.ds(0, HALO)] = jnp.where(tm == 0, jnp.zeros((HALO, n_cols), BF16), ext[pl.ds(0, HALO)])
    filtered[pl.ds(0, GAUGE_MAX)] = dot(toeplitz[:GAUGE_MAX, :HALO], ext[pl.ds(0, HALO)])
    fir(jnp.int32(0))

    rows = BLOCK + GAUGE_MAX
    masks = []
    for tile in range(n_tiles):
        lag = lag_ref[:, tile * 128:(tile + 1) * 128] - 1
        masks.append([lax.rem(lag // (2**b), 2) == 1 for b in range(4)])

    @pl.loop(0, n_blocks)
    def _(block):
        start = pl.multiple_of(block * BLOCK, BLOCK)
        for tile in range(n_tiles):
            cols = slice(tile * 128, (tile + 1) * 128)
            x = filtered[pl.ds(start, rows), cols]
            y = pltpu.roll(x, 1, 0)
            for b in (3, 2, 1, 0):
                y = jnp.where(jnp.broadcast_to(masks[tile][b], (rows, 128)), pltpu.roll(y, 2**b, 0), y)
            strain[pl.ds(start, BLOCK), cols] = (x - y)[GAUGE_MAX:].astype(BF16)

    stk[0, 0:RANK] = dot(proj_ref[...], strain[...], TN)

    def exchange(level):
        copy = pltpu.make_async_remote_copy(
            src_ref=stk.at[level, pl.ds(0, RANK)], dst_ref=stk.at[level, pl.ds(RANK, RANK)],
            send_sem=ex_sem.at[0, level], recv_sem=ex_sem.at[1, level],
            device_id={"tm": partners[level]}, device_id_type=MESH)
        copy.start()
        return copy

    def send_diag(level):
        copy = pltpu.make_async_remote_copy(
            src_ref=diag.at[level, 0], dst_ref=diag.at[level, 1],
            send_sem=dg_sem.at[0, level], recv_sem=dg_sem.at[1, level],
            device_id={"tm": partners[level]}, device_id_type=MESH)
        copy.start()
        return copy

    def scatter(j, value):
        value = value.reshape(n_chan, slice_rows, RANK)
        part[j] = value
        scat[j, me] = part[j, me]
        copies = []
        for o in offsets:
            peer = lax.rem(me + o, n_chan)
            copy = pltpu.make_async_remote_copy(
                src_ref=part.at[j, peer], dst_ref=scat.at[j, me],
                send_sem=rs_send.at[j, o], recv_sem=rs_recv.at[j, o],
                device_id={"chan": peer}, device_id_type=MESH)
            copy.start()
            copies.append(copy)
        return copies

    def gather(j, copies):
        for copy in copies:
            copy.wait()
        gath[j, me] = jnp.sum(scat[j], axis=0)
        copies = []
        for o in offsets:
            peer = lax.rem(me + o, n_chan)
            copy = pltpu.make_async_remote_copy(
                src_ref=gath.at[j, me], dst_ref=gath.at[j, me],
                send_sem=ag_send.at[j, o], recv_sem=ag_recv.at[j, o],
                device_id={"chan": peer}, device_id_type=MESH)
            copy.start()
            copies.append(copy)
        return copies

    def finish(j, copies):
        for copy in copies:
            copy.wait()
        return gath[j].reshape(RANK, RANK)

    eye = (lax.broadcasted_iota(jnp.int32, (2 * RANK, 2 * RANK), 0)
           == lax.broadcasted_iota(jnp.int32, (2 * RANK, 2 * RANK), 1)).astype(F32)

    def split_rows(level, low):
        high, rest = split(stk[level, low:low + RANK])
        stk_hi[low:low + RANK] = high
        stk_lo[low:low + RANK] = rest
        return high, rest

    diag_copy = None
    for level in range(levels):
        moving = exchange(level)
        own = split_rows(level, 0)
        if level == 0:
            diag_moving = scatter(levels, dot3(own, own, NT))
        else:
            mix, whole = split(a_ref_mix), split(gram[...])
            diag[level, 0] = dot3(split(dot3(mix, whole)), mix, NT)
            diag_copy = send_diag(level)
        moving.wait()
        other = split_rows(level, RANK)
        cross_moving = scatter(level, dot3(own, other, NT))
        if level == 0:
            diag_moving = gather(levels, diag_moving)
        cross_moving = gather(level, cross_moving)
        if level == 0:
            diag[level, 0] = finish(levels, diag_moving)
            diag_copy = send_diag(level)
        cross = finish(level, cross_moving)
        gram[0:RANK, RANK:] = cross
        gram[RANK:, 0:RANK] = cross.T
        gram[0:RANK, 0:RANK] = diag[level, 0]
        diag_copy.wait()
        gram[RANK:, RANK:] = diag[level, 1]

        value = gram[...]
        mean = jnp.sum(value * eye, keepdims=True) / (2 * RANK)
        shifted = value - mean * eye
        z_ref[...] = shifted / jnp.sqrt(jnp.sum(shifted * shifted, keepdims=True) + 1e-06)

        @pl.loop(0, K_ITERS)
        def _(step):
            z = split(z_ref[...])
            poly = 1.5 * eye - 0.5 * dot3(z, z)
            z_ref[...] = dot3(z, split(poly))

        upper = lax.rem(tm // 2**level, 2)
        if level < levels - 1:
            mine = comp_t[upper]
            mix_value = 0.5 * (mine + dot3(split(mine), split(z_ref[...])))
            a_ref_mix = mix_value
            mix = split(mix_value)
            stk[level + 1, 0:RANK] = dot3(mix, (stk_hi[...], stk_lo[...]))
        else:
            share = RANK // n_tm
            group = max(8, share)
            start = pl.multiple_of(tm * share // group * group, 8)
            mine = comp_t[upper, pl.ds(start, group)]
            mix = split(0.5 * (mine + dot3(split(mine), split(z_ref[...]))))
            result = dot3(mix, (stk_hi[...], stk_lo[...]))
            place = lax.rem(tm, group // share)
            picked = result[0:share]
            for i in range(1, group // share):
                picked = jnp.where(place == i, result[i * share:(i + 1) * share], picked)
            out_ref[...] = picked


def on_device(n_tm, n_chan, record, fir_taps, gauge_lag, projector, compress):
    n_rows, n_cols = record.shape
    levels = n_tm.bit_length() - 1
    base = lax.pad(lax.rev(fir_taps.astype(F32), (0,)), jnp.float32(0), ((1, 255 - TAPS, 0),)).reshape(1, 256)
    lag = gauge_lag.reshape(1, n_cols)
    slice_rows = RANK // n_chan
    dma = pltpu.SemaphoreType.DMA
    vmem = pl.BlockSpec(memory_space=pltpu.VMEM)
    return pl.pallas_call(
        functools.partial(kernel, n_tm, n_chan, levels),
        out_shape=jax.ShapeDtypeStruct((RANK // n_tm, n_cols), F32),
        in_specs=[pl.BlockSpec(memory_space=pl.ANY), vmem, vmem, vmem, vmem],
        out_specs=vmem,
        scratch_shapes=[
            pltpu.VMEM((HALO + n_rows, n_cols), BF16),
            pltpu.VMEM((GAUGE_MAX + n_rows, n_cols), F32),
            pltpu.VMEM((n_rows, n_cols), BF16),
            pltpu.VMEM((levels, 2 * RANK, n_cols), F32),
            pltpu.VMEM((2 * RANK, n_cols), BF16),
            pltpu.VMEM((2 * RANK, n_cols), BF16),
            pltpu.VMEM((2 * RANK, 2 * RANK), F32),
            pltpu.VMEM((levels, 2, RANK, RANK), F32),
            pltpu.VMEM((2, RANK, 2 * RANK), F32),
            pltpu.VMEM((levels + 1, n_chan, slice_rows, RANK), F32),
            pltpu.VMEM((levels + 1, n_chan, slice_rows, RANK), F32),
            pltpu.VMEM((levels + 1, n_chan, slice_rows, RANK), F32),
            pltpu.VMEM((2 * RANK, 2 * RANK), F32),
            pltpu.VMEM((2 * RANK, 6 * RANK), BF16),
            pltpu.VMEM((6 * RANK, 2 * RANK), BF16),
            dma,
            dma((2,)),
            dma((2, levels)),
            dma((2, levels)),
            dma((levels + 1, n_chan)),
            dma((levels + 1, n_chan)),
            dma((levels + 1, n_chan)),
            dma((levels + 1, n_chan)),
        ],
        compiler_params=pltpu.CompilerParams(collective_id=0, has_side_effects=True, vmem_limit_bytes=40 * 2**20),
    )(record, base, lag, projector, compress)


def solution(mesh):
    return jax.shard_map(
        functools.partial(on_device, mesh.shape["tm"], mesh.shape["chan"]),
        mesh=mesh,
        in_specs=(P("tm", "chan"), P(), P("chan"), P("tm", None), P()),
        out_specs=P("tm", "chan"),
        check_vma=False,
    )
```

time: 809 us -> 176 us (0.22)
  waiting for transfers between devices: 633 us -> 0 us
  Pallas kernels: 0 us -> 170 us
  matrix products: 81.5 us -> 0 us
  starting transfers between devices: 27.5 us -> 0 us
  other arithmetic: 21.4 us -> 0 us
  between operations: 21.3 us -> 0.01 us
  local copies, waits for them, and re-layouts: 13.8 us -> 5.28 us
    psum x5 -> x0, waiting for transfers between devices: 590 us -> none  [on_device(): gram = lax.psum(inner_rows(stacked, stacked), 'chan')]
    pallas_call x0 -> x1, Pallas kernels: none -> 170 us  [on_device(): pl.pallas_call(functools.partial(kernel, n_tm, n_chan, levels), out_shape...]
    dot_general x105 -> x0, matrix products: 81.5 us -> none  [the longest x1 24.8 us: on_device(): lax.dot_general(projector, strain, (((0,), (0,)), ((), ())), preferred_el...]
    ppermute x6 -> x0, waiting for transfers between devices: 42.9 us -> none  [the longest x5 42.9 us: from_partner(): return lax.ppermute(value, axis, pairs)]
    ppermute x6 -> x0, starting transfers between devices: 26.2 us -> none  [the longest x5 22.3 us: from_partner(): return lax.ppermute(value, axis, pairs)]
    reduce_sum x12 -> x0, other arithmetic: 18.3 us -> none  [the longest x5 8.13 us: filter_mix(): signed = shifted / jnp.sqrt(jnp.sum(shifted * shifted) + 1e-06)]
  transfers between devices with their start and end apart: 11 -> 0, of which waited for: 10 -> 0; matrix products, arithmetic and copies ran while one was open for 0% -> 0% of each run, Pallas kernels for 0% -> 0%
where the time goes in v1:
time: 176 us
  Pallas kernels  170 us (97%)
  local copies, waits for them, and re-layouts  5.28 us (3%)
    pallas_call x1, Pallas kernels, on_device(): pl.pallas_call(functools.partial(kernel, n_tm, n_chan, levels), out_shape...  170 us
    unnamed x7, local copies, waits for them, and re-layouts  3.77 us

profile of v1, /device:TPU:1, one launch (start us, length us, event | category | flops | bytes accessed | tf_op | source)
XLA Modules:
  0.0 175.6 jit_solution(11272389909923389095)
XLA Ops:
  0.0 0.7 rev.3
  0.7 0.1 pad.3
  0.8 0.7 reshape.7.lag_ref
  1.5 0.0 copy-start
  1.5 1.3 copy-done
  2.8 0.0 copy-start.1
  2.8 0.9 copy-done.1
  3.8 0.0 copy-start.2
  3.8 0.9 copy-done.2
  4.7 170.3 %shard_map.55 = f32[4,640]{1,0:T(4,128)S(1)} custom-call(bf16[1024,640]{1,0:T(8,128)(2,1)S(1)} %copy-done, f32[1,256]{1,0:T(1,128)S(1)} %bitcast.1, s32[1,640]{1,0:T(1,128)S(1)} %reshape.7.lag_ref, bf16[1024,128]{1,0:T(8,128)(2,1)S(1)} %copy-done.1, f32[256,128]{1,0:T(8,128)S(1)} %copy-done.2), custom_call_target="tpu_custom_call" | custom-call | tf_op jit(solution)/shard_map/pallas_call | solution.py:240
  175.0 0.6 copy.7
Async XLA Ops:
  1.5 1.3 copy-start
  2.8 0.9 copy-start.1
  3.8 0.9 copy-start.2

commit v2 on v1

v2 whole, which is shorter than its diff:
```python
import functools

import jax
import jax.numpy as jnp
from jax import lax
from jax.experimental import pallas as pl
from jax.experimental.pallas import tpu as pltpu
from jax.sharding import PartitionSpec as P

TAPS = 64
GAUGE_MAX = 16
K_ITERS = 8
HALO = 80
RANK = 128
BLOCK = 128
MOST = 8
MESH = pl.DeviceIdType.MESH
F32 = jnp.float32
BF16 = jnp.bfloat16


def split(value):
    high = value.astype(BF16)
    return high, (value - high.astype(F32)).astype(BF16)


def dot(first, second, contract=((1,), (0,))):
    return lax.dot_general(first, second, (contract, ((), ())), preferred_element_type=F32)


def dot3(first, second, contract=((1,), (0,))):
    fh, fl = first
    sh, sl = second
    return dot(fh, sh, contract) + (dot(fh, sl, contract) + dot(fl, sh, contract))


NT = ((1,), (1,))
TN = ((0,), (0,))


def kernel(n_tm, n_chan, levels, record, base_ref, lag_ref, proj_hbm, comp_hbm, out_ref,
           ext, filtered, strain, proj_ref, comp_ref, stk, stk_hi, stk_lo, gram, diag, comp_t, part, scat, gath,
           crossp, pre, zbuf, cross, give, take, mix_hi, mix_lo,
           local_sem, halo_sem, ex_sem, dg_sem, rs_send, rs_recv, ag_send, ag_recv,
           pre_sem, z_send, z_recv, g_send, g_recv, f_send, f_recv, last_sem):
    tm = lax.axis_index("tm")
    me = lax.axis_index("chan")
    n_rows, n_cols = record.shape
    slice_rows = RANK // n_chan
    n_blocks = n_rows // BLOCK
    n_tiles = n_cols // 128
    n_z = n_chan // 2
    core = lax.rem(me, 2)
    z_me = me // 2
    other_core = me + 1 - 2 * core

    load = pltpu.make_async_copy(record, ext.at[pl.ds(HALO, n_rows)], local_sem.at[0])
    load_proj = pltpu.make_async_copy(proj_hbm, proj_ref, local_sem.at[1])
    load_comp = pltpu.make_async_copy(comp_hbm, comp_ref, local_sem.at[2])
    load.start()
    load_proj.start()
    load_comp.start()

    nxt = lax.rem(tm + 1, n_tm)
    prv = lax.rem(tm + n_tm - 1, n_tm)
    partners = []
    for level in range(levels):
        bit = 2**level
        partners.append(tm + bit * (1 - 2 * lax.rem(tm // bit, 2)))
    offsets = sorted(range(1, n_chan), key=lambda o: -min(o, n_chan - o))
    z_offsets = sorted(range(1, n_z), key=lambda o: -min(o, n_z - o))
    most = min(MOST, n_tm)

    def member(count, i):
        return tm // count * count + lax.rem(tm + i, count)

    barrier = pltpu.get_barrier_semaphore()
    greeted = [{"tm": nxt}, {"tm": prv}]
    greeted += [{"tm": partners[level]} for level in range(levels) if 2**level >= most]
    greeted += [{"chan": lax.rem(me + o, n_chan)} for o in offsets]
    greeted += [{"tm": member(most, i), "chan": c} for i in range(1, most) for c in (me, other_core)]
    for who in greeted:
        pl.semaphore_signal(barrier, inc=1, device_id=who, device_id_type=MESH)
    pl.semaphore_wait(barrier, len(greeted))

    halo = pltpu.make_async_remote_copy(
        src_ref=record.at[pl.ds(n_rows - HALO, HALO)], dst_ref=ext.at[pl.ds(0, HALO)],
        send_sem=halo_sem.at[0], recv_sem=halo_sem.at[1], device_id={"tm": nxt}, device_id_type=MESH)
    halo.start()

    toeplitz = pltpu.roll(jnp.broadcast_to(base_ref[...], (BLOCK, 256)), 0, 1, stride=1, stride_axis=0)
    toeplitz = toeplitz[:, :BLOCK + TAPS].astype(BF16)
    load.wait()

    def fir(block):
        start = block * BLOCK
        window = ext[start + GAUGE_MAX:start + GAUGE_MAX + BLOCK + TAPS]
        filtered[start + GAUGE_MAX:start + GAUGE_MAX + BLOCK] = dot(toeplitz, window)

    masks = []
    for tile in range(n_tiles):
        lag = lag_ref[:, tile * 128:(tile + 1) * 128] - 1
        masks.append([lax.rem(lag // (2**b), 2) == 1 for b in range(4)])

    rows = BLOCK + GAUGE_MAX

    def difference(block):
        start = pl.multiple_of(block * BLOCK, BLOCK)
        for tile in range(n_tiles):
            cols = slice(tile * 128, (tile + 1) * 128)
            x = filtered[pl.ds(start, rows), cols]
            y = pltpu.roll(x, 1, 0)
            for b in (3, 2, 1, 0):
                y = jnp.where(jnp.broadcast_to(masks[tile][b], (rows, 128)), pltpu.roll(y, 2**b, 0), y)
            strain[pl.ds(start, BLOCK), cols] = (x - y)[GAUGE_MAX:].astype(BF16)

    for block in range(1, n_blocks):
        fir(block)

    @pl.loop(2, n_blocks)
    def _(block):
        difference(block)

    halo.wait()
    ext[pl.ds(0, HALO)] = jnp.where(tm == 0, jnp.zeros((HALO, n_cols), BF16), ext[pl.ds(0, HALO)])
    filtered[pl.ds(0, GAUGE_MAX)] = dot(toeplitz[:GAUGE_MAX, :HALO], ext[pl.ds(0, HALO)])
    fir(0)

    @pl.loop(0, 2)
    def _(block):
        difference(block)

    load_proj.wait()
    stk[0, 0:RANK] = dot(proj_ref[...], strain[...], TN)

    def remote(src, dst, send_sem, recv_sem, who):
        copy = pltpu.make_async_remote_copy(
            src_ref=src, dst_ref=dst, send_sem=send_sem, recv_sem=recv_sem, device_id=who, device_id_type=MESH)
        copy.start()
        return copy

    def send_diag(level):
        return remote(diag.at[level, 0], diag.at[level, 1], dg_sem.at[0, level], dg_sem.at[1, level],
                      {"tm": partners[level]})

    def scatter(j, value):
        part[j] = value.reshape(n_chan, slice_rows, RANK)
        scat[j, me] = part[j, me]
        copies = []
        for o in offsets:
            peer = lax.rem(me + o, n_chan)
            copies.append(remote(part.at[j, peer], scat.at[j, me], rs_send.at[j, o], rs_recv.at[j, o], {"chan": peer}))
        return copies

    def gather(j, copies):
        for copy in copies:
            copy.wait()
        gath[j, me] = jnp.sum(scat[j], axis=0)
        copies = []
        for o in offsets:
            peer = lax.rem(me + o, n_chan)
            copies.append(remote(gath.at[j, me], gath.at[j, me], ag_send.at[j, o], ag_recv.at[j, o], {"chan": peer}))
        return copies

    def finish(j, copies):
        for copy in copies:
            copy.wait()
        return gath[j].reshape(RANK, RANK)

    eye = (lax.broadcasted_iota(jnp.int32, (2 * RANK, 2 * RANK), 0)
           == lax.broadcasted_iota(jnp.int32, (2 * RANK, 2 * RANK), 1)).astype(F32)

    def split_rows(level, low, count):
        high, rest = split(stk[level, low:low + count])
        stk_hi[low:low + count] = high
        stk_lo[low:low + count] = rest
        return high, rest

    for level in range(levels):
        count = min(2**level, most)
        r = RANK // count
        h = r // 2
        last = level == levels - 1
        place = lax.rem(tm, count)
        mine_rows = pl.ds(pl.multiple_of(place * r, 8), r)
        got_rows = pl.ds(pl.multiple_of(RANK + place * r, 8), r)
        moving = remote(stk.at[level, mine_rows], stk.at[level, got_rows], ex_sem.at[0, level], ex_sem.at[1, level],
                        {"tm": partners[level]})
        own = split_rows(level, 0, RANK)
        if level == 0:
            diag_moving = scatter(0, dot3(own, own, NT))
            load_comp.wait()
            comp = comp_ref[...].T
            comp_t[0] = comp
            comp_t[1, :, 0:RANK] = comp[:, RANK:]
            comp_t[1, :, RANK:] = comp[:, :RANK]
            diag_moving = gather(0, diag_moving)
            moving.wait()
            cross_moving = scatter(1, dot3(split_rows(0, RANK, RANK), own, NT))
            diag[0, 0] = finish(0, diag_moving)
            diag_copy = send_diag(0)
            cross_moving = gather(1, cross_moving)
            below = finish(1, cross_moving)
        else:
            mix = (mix_hi[...], mix_lo[...])
            diag[level, 0] = dot3(split(dot3(mix, split(gram[...]))), mix, NT)
            diag_copy = send_diag(level)
            moving.wait()
            crossp[level, 0:r] = dot3(split(stk[level, got_rows]), own, NT)
            half = pl.ds(pl.multiple_of(core * h, 8), h)
            away = pl.ds(pl.multiple_of((1 - core) * h, 8), h)
            pre_copy = remote(crossp.at[level, away], pre.at[level, pl.ds(0, h)], pre_sem.at[0, level], pre_sem.at[1, level],
                              {"chan": other_core})
            forwards = []
            if not last:
                for i in range(1, count):
                    forwards.append(remote(stk.at[level, got_rows], stk.at[level, got_rows],
                                           f_send.at[level, i], f_recv.at[level, i], {"tm": member(count, i)}))
            pre_copy.wait()
            slot = zbuf.at[level, z_me, pl.ds(0, h)]
            slot[...] = crossp[level, half] + pre[level, 0:h]
            copies = []
            for o in z_offsets:
                peer = lax.rem(me + 2 * o, n_chan)
                copies.append(remote(slot, slot, z_send.at[level, o], z_recv.at[level, o], {"chan": peer}))
            for copy in copies:
                copy.wait()
            chunk = cross.at[level, pl.ds(pl.multiple_of(place * r + core * h, 8), h)]
            chunk[...] = jnp.sum(zbuf[level, :, 0:h], axis=0)
            copies = []
            for i in range(count - 1, -1, -1):
                for d in range(2):
                    if i + d > 0:
                        who = {"tm": member(count, i), "chan": me if d == 0 else other_core}
                        copies.append(remote(chunk, chunk, g_send.at[level, 2 * i + d], g_recv.at[level, 2 * i + d], who))
            for copy in forwards:
                copy.wait()
            if not last:
                split_rows(level, RANK, RANK)
            for copy in copies:
                copy.wait()
            below = cross[level]

        gram[RANK:, 0:RANK] = below
        gram[0:RANK, RANK:] = below.T
        gram[0:RANK, 0:RANK] = diag[level, 0]
        diag_copy.wait()
        gram[RANK:, RANK:] = diag[level, 1]

        value = gram[...]
        mean = jnp.sum(value * eye, keepdims=True) / (2 * RANK)
        shifted = value - mean * eye
        z = shifted / jnp.sqrt(jnp.sum(shifted * shifted, keepdims=True) + 1e-06)
        for step in range(K_ITERS):
            parts = split(z)
            z = 1.5 * z - 0.5 * dot3(parts, split(dot3(parts, parts)))

        upper = lax.rem(tm // 2**level, 2)
        if not last:
            mine = comp_t[upper]
            mix = split(0.5 * (mine + dot3(split(mine), split(z))))
            mix_hi[...], mix_lo[...] = mix
            stk[level + 1, 0:RANK] = dot3(mix, (stk_hi[...], stk_lo[...]))
        else:
            share = RANK // n_tm
            group = max(8, share)
            wanted = [comp_t[upper, pl.ds(pl.multiple_of(who * share // group * group, 8), group)]
                      for who in (tm, partners[level])]
            wanted = jnp.concatenate(wanted, 0)
            high, rest = split(z[:, 0:RANK])
            mix = split(0.5 * (wanted[:, 0:RANK] + dot3(split(wanted), (high, rest))))
            result = dot3(mix, own)

            def pick(block, who):
                spot = lax.rem(who, group // share)
                chosen = block[0:share]
                for i in range(1, group // share):
                    chosen = jnp.where(spot == i, block[i * share:(i + 1) * share], chosen)
                return chosen

            give[...] = pick(result[group:], partners[level])
            final = remote(give, take, last_sem.at[0], last_sem.at[1], {"tm": partners[level]})
            kept = pick(result[:group], tm)
            final.wait()
            out_ref[...] = kept + take[...]


def on_device(n_tm, n_chan, record, fir_taps, gauge_lag, projector, compress):
    n_rows, n_cols = record.shape
    levels = n_tm.bit_length() - 1
    base = lax.pad(lax.rev(fir_taps.astype(F32), (0,)), jnp.float32(0), ((1, 255 - TAPS, 0),)).reshape(1, 256)
    lag = gauge_lag.reshape(1, n_cols)
    slice_rows = RANK // n_chan
    most = min(MOST, n_tm)
    dma = pltpu.SemaphoreType.DMA
    vmem = pl.BlockSpec(memory_space=pltpu.VMEM)
    hbm = pl.BlockSpec(memory_space=pltpu.HBM)
    return pl.pallas_call(
        functools.partial(kernel, n_tm, n_chan, levels),
        out_shape=jax.ShapeDtypeStruct((RANK // n_tm, n_cols), F32),
        in_specs=[hbm, vmem, vmem, hbm, hbm],
        out_specs=vmem,
        scratch_shapes=[
            pltpu.VMEM((HALO + n_rows, n_cols), BF16),
            pltpu.VMEM((GAUGE_MAX + n_rows, n_cols), F32),
            pltpu.VMEM((n_rows, n_cols), BF16),
            pltpu.VMEM((n_rows, RANK), BF16),
            pltpu.VMEM((2 * RANK, RANK), F32),
            pltpu.VMEM((levels, 2 * RANK, n_cols), F32),
            pltpu.VMEM((2 * RANK, n_cols), BF16),
            pltpu.VMEM((2 * RANK, n_cols), BF16),
            pltpu.VMEM((2 * RANK, 2 * RANK), F32),
            pltpu.VMEM((levels, 2, RANK, RANK), F32),
            pltpu.VMEM((2, RANK, 2 * RANK), F32),
            pltpu.VMEM((2, n_chan, slice_rows, RANK), F32),
            pltpu.VMEM((2, n_chan, slice_rows, RANK), F32),
            pltpu.VMEM((2, n_chan, slice_rows, RANK), F32),
            pltpu.VMEM((levels, RANK // 2, RANK), F32),
            pltpu.VMEM((levels, RANK // 4, RANK), F32),
            pltpu.VMEM((levels, n_chan // 2, RANK // 4, RANK), F32),
            pltpu.VMEM((levels, RANK, RANK), F32),
            pltpu.VMEM((RANK // n_tm, n_cols), F32),
            pltpu.VMEM((RANK // n_tm, n_cols), F32),
            pltpu.VMEM((RANK, 2 * RANK), BF16),
            pltpu.VMEM((RANK, 2 * RANK), BF16),
            dma((3,)),
            dma((2,)),
            dma((2, levels)),
            dma((2, levels)),
            dma((2, n_chan)),
            dma((2, n_chan)),
            dma((2, n_chan)),
            dma((2, n_chan)),
            dma((2, levels)),
            dma((levels, n_chan // 2)),
            dma((levels, n_chan // 2)),
            dma((levels, 2 * most)),
            dma((levels, 2 * most)),
            dma((levels, most)),
            dma((levels, most)),
            dma((2,)),
        ],
        compiler_params=pltpu.CompilerParams(collective_id=0, has_side_effects=True, vmem_limit_bytes=40 * 2**20),
    )(record, base, lag, projector, compress)


def solution(mesh):
    return jax.shard_map(
        functools.partial(on_device, mesh.shape["tm"], mesh.shape["chan"]),
        mesh=mesh,
        in_specs=(P("tm", "chan"), P(), P("chan"), P("tm", None), P()),
        out_specs=P("tm", "chan"),
        check_vma=False,
    )
```

time: 176 us -> 148 us (0.84)
  Pallas kernels: 170 us -> 142 us
    pallas_call x1, Pallas kernels: 170 us -> 142 us  [on_device(): pl.pallas_call(functools.partial(kernel, n_tm, n_chan, levels), out_shape...]
where the time goes in v2:
time: 148 us; the launch traced here: 147 us
  Pallas kernels  142 us (96%)
  local copies, waits for them, and re-layouts  5.28 us (4%)
    pallas_call x1, Pallas kernels, on_device(): pl.pallas_call(functools.partial(kernel, n_tm, n_chan, levels), out_shape...  142 us
    unnamed x7, local copies, waits for them, and re-layouts  3.77 us

profile of v2, /device:TPU:1, one launch (start us, length us, event | category | flops | bytes accessed | tf_op | source)
XLA Modules:
  0.0 147.3 jit_solution(14849753505901851293)
XLA Ops:
  0.0 0.7 rev.3
  0.7 0.1 pad.3
  0.8 0.7 reshape.7.lag_ref
  1.5 0.0 copy-start
  1.5 1.3 copy-done
  2.8 0.0 copy-start.1
  2.8 0.9 copy-done.1
  3.8 0.0 copy-start.2
  3.8 0.9 copy-done.2
  4.7 142.0 %shard_map.55 = f32[4,640]{1,0:T(4,128)S(1)} custom-call(bf16[1024,640]{1,0:T(8,128)(2,1)S(1)} %copy-done, f32[1,256]{1,0:T(1,128)S(1)} %bitcast.1, s32[1,640]{1,0:T(1,128)S(1)} %reshape.7.lag_ref, bf16[1024,128]{1,0:T(8,128)(2,1)S(1)} %copy-done.1, f32[256,128]{1,0:T(8,128)S(1)} %copy-done.2), custom_call_target="tpu_custom_call" | custom-call | tf_op jit(solution)/shard_map/pallas_call | solution.py:298
  146.7 0.6 copy.7
Async XLA Ops:
  1.5 1.3 copy-start
  2.8 0.9 copy-start.1
  3.8 0.9 copy-start.2

commit v3 on v2

--- a/solution.py
+++ b/solution.py
@@ -38,11 +38,11 @@
 TN = ((0,), (0,))
 
 
-def kernel(n_tm, n_chan, levels, record, base_ref, lag_ref, proj_hbm, comp_hbm, out_ref,
-           ext, filtered, strain, proj_ref, comp_ref, stk, stk_hi, stk_lo, gram, diag, comp_t, part, scat, gath,
-           crossp, pre, zbuf, cross, give, take, mix_hi, mix_lo,
+def kernel(n_tm, n_chan, levels, record, taps_hbm, lag_hbm, proj_hbm, comp_hbm, out_ref,
+           ext, filtered, strain, proj_ref, comp_ref, taps_ref, lag_ref, stk, stk_hi, stk_lo, gram, diag, comp_t, part, scat, gath,
+           crossp, pre, zbuf, cross, ahead, mix_hi, mix_lo,
            local_sem, halo_sem, ex_sem, dg_sem, rs_send, rs_recv, ag_send, ag_recv,
-           pre_sem, z_send, z_recv, g_send, g_recv, f_send, f_recv, last_sem):
+           pre_sem, z_send, z_recv, g_send, g_recv, f_send, f_recv):
     tm = lax.axis_index("tm")
     me = lax.axis_index("chan")
     n_rows, n_cols = record.shape
@@ -57,6 +57,10 @@
     load = pltpu.make_async_copy(record, ext.at[pl.ds(HALO, n_rows)], local_sem.at[0])
     load_proj = pltpu.make_async_copy(proj_hbm, proj_ref, local_sem.at[1])
     load_comp = pltpu.make_async_copy(comp_hbm, comp_ref, local_sem.at[2])
+    load_taps = pltpu.make_async_copy(taps_hbm, taps_ref, local_sem.at[3])
+    load_lag = pltpu.make_async_copy(lag_hbm, lag_ref, local_sem.at[4])
+    load_taps.start()
+    load_lag.start()
     load.start()
     load_proj.start()
     load_comp.start()
@@ -81,15 +85,12 @@
     greeted += [{"tm": member(most, i), "chan": c} for i in range(1, most) for c in (me, other_core)]
     for who in greeted:
         pl.semaphore_signal(barrier, inc=1, device_id=who, device_id_type=MESH)
-    pl.semaphore_wait(barrier, len(greeted))
-
-    halo = pltpu.make_async_remote_copy(
-        src_ref=record.at[pl.ds(n_rows - HALO, HALO)], dst_ref=ext.at[pl.ds(0, HALO)],
-        send_sem=halo_sem.at[0], recv_sem=halo_sem.at[1], device_id={"tm": nxt}, device_id_type=MESH)
-    halo.start()
-
-    toeplitz = pltpu.roll(jnp.broadcast_to(base_ref[...], (BLOCK, 256)), 0, 1, stride=1, stride_axis=0)
-    toeplitz = toeplitz[:, :BLOCK + TAPS].astype(BF16)
+
+    load_taps.wait()
+    load_lag.wait()
+    taps = jnp.concatenate([taps_ref[...].astype(F32).reshape(1, TAPS), jnp.zeros((1, 256 - TAPS), F32)], 1)
+    banded = pltpu.roll(jnp.broadcast_to(taps, (BLOCK + TAPS, 256)), 256 - TAPS, 1, stride=1, stride_axis=0)
+    toeplitz = banded[:, 0:BLOCK].T.astype(BF16)
     load.wait()
 
     def fir(block):
@@ -99,7 +100,7 @@
 
     masks = []
     for tile in range(n_tiles):
-        lag = lag_ref[:, tile * 128:(tile + 1) * 128] - 1
+        lag = lag_ref[tile * 128:(tile + 1) * 128].reshape(1, 128) - 1
         masks.append([lax.rem(lag // (2**b), 2) == 1 for b in range(4)])
 
     rows = BLOCK + GAUGE_MAX
@@ -121,6 +122,19 @@
     def _(block):
         difference(block)
 
+    pl.semaphore_wait(barrier, len(greeted))
+    halo = pltpu.make_async_remote_copy(
+        src_ref=record.at[pl.ds(n_rows - HALO, HALO)], dst_ref=ext.at[pl.ds(0, HALO)],
+        send_sem=halo_sem.at[0], recv_sem=halo_sem.at[1], device_id={"tm": nxt}, device_id_type=MESH)
+    halo.start()
+    load_proj.wait()
+    late = 2 * BLOCK
+    stk[0, 0:RANK] = dot(proj_ref[late:], strain[late:], TN)
+    load_comp.wait()
+    comp = comp_ref[...].T
+    comp_t[0] = comp
+    comp_t[1, :, 0:RANK] = comp[:, RANK:]
+    comp_t[1, :, RANK:] = comp[:, :RANK]
     halo.wait()
     ext[pl.ds(0, HALO)] = jnp.where(tm == 0, jnp.zeros((HALO, n_cols), BF16), ext[pl.ds(0, HALO)])
     filtered[pl.ds(0, GAUGE_MAX)] = dot(toeplitz[:GAUGE_MAX, :HALO], ext[pl.ds(0, HALO)])
@@ -130,8 +144,7 @@
     def _(block):
         difference(block)
 
-    load_proj.wait()
-    stk[0, 0:RANK] = dot(proj_ref[...], strain[...], TN)
+    stk[0, 0:RANK] += dot(proj_ref[0:late], strain[0:late], TN)
 
     def remote(src, dst, send_sem, recv_sem, who):
         copy = pltpu.make_async_remote_copy(
@@ -182,18 +195,13 @@
         h = r // 2
         last = level == levels - 1
         place = lax.rem(tm, count)
-        mine_rows = pl.ds(pl.multiple_of(place * r, 8), r)
         got_rows = pl.ds(pl.multiple_of(RANK + place * r, 8), r)
-        moving = remote(stk.at[level, mine_rows], stk.at[level, got_rows], ex_sem.at[0, level], ex_sem.at[1, level],
-                        {"tm": partners[level]})
+        if level == 0:
+            moving = remote(stk.at[0, pl.ds(0, RANK)], stk.at[0, pl.ds(RANK, RANK)], ex_sem.at[0, 0], ex_sem.at[1, 0],
+                            {"tm": partners[0]})
         own = split_rows(level, 0, RANK)
         if level == 0:
             diag_moving = scatter(0, dot3(own, own, NT))
-            load_comp.wait()
-            comp = comp_ref[...].T
-            comp_t[0] = comp
-            comp_t[1, :, 0:RANK] = comp[:, RANK:]
-            comp_t[1, :, RANK:] = comp[:, :RANK]
             diag_moving = gather(0, diag_moving)
             moving.wait()
             cross_moving = scatter(1, dot3(split_rows(0, RANK, RANK), own, NT))
@@ -212,10 +220,9 @@
             pre_copy = remote(crossp.at[level, away], pre.at[level, pl.ds(0, h)], pre_sem.at[0, level], pre_sem.at[1, level],
                               {"chan": other_core})
             forwards = []
-            if not last:
-                for i in range(1, count):
-                    forwards.append(remote(stk.at[level, got_rows], stk.at[level, got_rows],
-                                           f_send.at[level, i], f_recv.at[level, i], {"tm": member(count, i)}))
+            for i in range(1, count):
+                forwards.append(remote(stk.at[level, got_rows], stk.at[level, got_rows],
+                                       f_send.at[level, i], f_recv.at[level, i], {"tm": member(count, i)}))
             pre_copy.wait()
             slot = zbuf.at[level, z_me, pl.ds(0, h)]
             slot[...] = crossp[level, half] + pre[level, 0:h]
@@ -235,8 +242,7 @@
                         copies.append(remote(chunk, chunk, g_send.at[level, 2 * i + d], g_recv.at[level, 2 * i + d], who))
             for copy in forwards:
                 copy.wait()
-            if not last:
-                split_rows(level, RANK, RANK)
+            split_rows(level, RANK, RANK)
             for copy in copies:
                 copy.wait()
             below = cross[level]
@@ -256,40 +262,38 @@
             z = 1.5 * z - 0.5 * dot3(parts, split(dot3(parts, parts)))
 
         upper = lax.rem(tm // 2**level, 2)
+        parts = split(z)
+        both = (stk_hi[...], stk_lo[...])
+
+        def mixed(rows):
+            mine = comp_t[upper, rows]
+            return split(0.5 * (mine + dot3(split(mine), parts)))
+
         if not last:
-            mine = comp_t[upper]
-            mix = split(0.5 * (mine + dot3(split(mine), split(z))))
+            after = min(2 * 2**level, most)
+            size = RANK // after
+            spot = lax.rem(tm, after) * size
+            ahead[level + 1, 0:size] = dot3(mixed(pl.ds(pl.multiple_of(spot, 8), size)), both)
+            moving = remote(ahead.at[level + 1, pl.ds(0, size)],
+                            stk.at[level + 1, pl.ds(pl.multiple_of(RANK + spot, 8), size)],
+                            ex_sem.at[0, level + 1], ex_sem.at[1, level + 1], {"tm": partners[level + 1]})
+            mix = mixed(pl.ds(0, RANK))
             mix_hi[...], mix_lo[...] = mix
-            stk[level + 1, 0:RANK] = dot3(mix, (stk_hi[...], stk_lo[...]))
+            stk[level + 1, 0:RANK] = dot3(mix, both)
         else:
             share = RANK // n_tm
             group = max(8, share)
-            wanted = [comp_t[upper, pl.ds(pl.multiple_of(who * share // group * group, 8), group)]
-                      for who in (tm, partners[level])]
-            wanted = jnp.concatenate(wanted, 0)
-            high, rest = split(z[:, 0:RANK])
-            mix = split(0.5 * (wanted[:, 0:RANK] + dot3(split(wanted), (high, rest))))
-            result = dot3(mix, own)
-
-            def pick(block, who):
-                spot = lax.rem(who, group // share)
-                chosen = block[0:share]
-                for i in range(1, group // share):
-                    chosen = jnp.where(spot == i, block[i * share:(i + 1) * share], chosen)
-                return chosen
-
-            give[...] = pick(result[group:], partners[level])
-            final = remote(give, take, last_sem.at[0], last_sem.at[1], {"tm": partners[level]})
-            kept = pick(result[:group], tm)
-            final.wait()
-            out_ref[...] = kept + take[...]
+            result = dot3(mixed(pl.ds(pl.multiple_of(tm * share // group * group, 8), group)), both)
+            spot = lax.rem(tm, group // share)
+            chosen = result[0:share]
+            for i in range(1, group // share):
+                chosen = jnp.where(spot == i, result[i * share:(i + 1) * share], chosen)
+            out_ref[...] = chosen
 
 
 def on_device(n_tm, n_chan, record, fir_taps, gauge_lag, projector, compress):
     n_rows, n_cols = record.shape
     levels = n_tm.bit_length() - 1
-    base = lax.pad(lax.rev(fir_taps.astype(F32), (0,)), jnp.float32(0), ((1, 255 - TAPS, 0),)).reshape(1, 256)
-    lag = gauge_lag.reshape(1, n_cols)
     slice_rows = RANK // n_chan
     most = min(MOST, n_tm)
     dma = pltpu.SemaphoreType.DMA
@@ -298,7 +302,7 @@
     return pl.pallas_call(
         functools.partial(kernel, n_tm, n_chan, levels),
         out_shape=jax.ShapeDtypeStruct((RANK // n_tm, n_cols), F32),
-        in_specs=[hbm, vmem, vmem, hbm, hbm],
+        in_specs=[hbm] * 5,
         out_specs=vmem,
         scratch_shapes=[
             pltpu.VMEM((HALO + n_rows, n_cols), BF16),
@@ -306,6 +310,8 @@
             pltpu.VMEM((n_rows, n_cols), BF16),
             pltpu.VMEM((n_rows, RANK), BF16),
             pltpu.VMEM((2 * RANK, RANK), F32),
+            pltpu.VMEM((TAPS,), BF16),
+            pltpu.VMEM((n_cols,), jnp.int32),
             pltpu.VMEM((levels, 2 * RANK, n_cols), F32),
             pltpu.VMEM((2 * RANK, n_cols), BF16),
             pltpu.VMEM((2 * RANK, n_cols), BF16),
@@ -319,11 +325,10 @@
             pltpu.VMEM((levels, RANK // 4, RANK), F32),
             pltpu.VMEM((levels, n_chan // 2, RANK // 4, RANK), F32),
             pltpu.VMEM((levels, RANK, RANK), F32),
-            pltpu.VMEM((RANK // n_tm, n_cols), F32),
-            pltpu.VMEM((RANK // n_tm, n_cols), F32),
+            pltpu.VMEM((levels, RANK // 2, n_cols), F32),
             pltpu.VMEM((RANK, 2 * RANK), BF16),
             pltpu.VMEM((RANK, 2 * RANK), BF16),
-            dma((3,)),
+            dma((5,)),
             dma((2,)),
             dma((2, levels)),
             dma((2, levels)),
@@ -338,10 +343,9 @@
             dma((levels, 2 * most)),
             dma((levels, most)),
             dma((levels, most)),
-            dma((2,)),
         ],
-        compiler_params=pltpu.CompilerParams(collective_id=0, has_side_effects=True, vmem_limit_bytes=40 * 2**20),
-    )(record, base, lag, projector, compress)
+        compiler_params=pltpu.CompilerParams(collective_id=0, has_side_effects=True, vmem_limit_bytes=67_000_000),
+    )(record, fir_taps, gauge_lag, projector, compress)
 
 
 def solution(mesh):

time: 148 us -> 140 us (0.946)
  Pallas kernels: 142 us -> 138 us
  local copies, waits for them, and re-layouts: 5.28 us -> 1.3 us
    pallas_call x1, Pallas kernels: 142 us -> 138 us  [on_device(): pl.pallas_call(functools.partial(kernel, n_tm, n_chan, levels), out_shape...]
    unnamed x7 -> x1, local copies, waits for them, and re-layouts: 3.77 us -> 1.3 us
where the time goes in v3:
time: 140 us
  Pallas kernels  138 us (99%)
    pallas_call x1, Pallas kernels, on_device(): pl.pallas_call(functools.partial(kernel, n_tm, n_chan, levels), out_shape...  138 us

profile of v3, /device:TPU:1, one launch (start us, length us, event | category | flops | bytes accessed | tf_op | source)
XLA Modules:
  0.0 139.6 jit_solution(4945011316714898473)
XLA Ops:
  0.0 138.3 %shard_map.55 = f32[4,640]{1,0:T(4,128)} custom-call(bf16[1024,640]{1,0:T(8,128)(2,1)} %record.1, bf16[64]{0:T(256)(128)(2,1)} %taps_hbm.1, s32[640]{0:T(1024)} %lag_hbm.1, bf16[1024,128]{1,0:T(8,128)(2,1)} %proj_hbm.1, f32[256,128]{1,0:T(8,128)} %comp_hbm.1), custom_call_target="tpu_custom_call" | custom-call | tf_op jit(solution)/shard_map/pallas_call | solution.py:302
  138.3 1.3 copy.7

commit v4 on v3

--- a/solution.py
+++ b/solution.py
@@ -14,6 +14,7 @@
 RANK = 128
 BLOCK = 128
 MOST = 8
+COARSE = 5
 MESH = pl.DeviceIdType.MESH
 F32 = jnp.float32
 BF16 = jnp.bfloat16
@@ -40,9 +41,9 @@
 
 def kernel(n_tm, n_chan, levels, record, taps_hbm, lag_hbm, proj_hbm, comp_hbm, out_ref,
            ext, filtered, strain, proj_ref, comp_ref, taps_ref, lag_ref, stk, stk_hi, stk_lo, gram, diag, comp_t, part, scat, gath,
-           crossp, pre, zbuf, cross, ahead, mix_hi, mix_lo,
+           crossp, pre, zbuf, wide, cross, ahead, mix_hi, mix_lo,
            local_sem, halo_sem, ex_sem, dg_sem, rs_send, rs_recv, ag_send, ag_recv,
-           pre_sem, z_send, z_recv, g_send, g_recv, f_send, f_recv):
+           pre_sem, z_send, z_recv, g_send, g_recv, f_send, f_recv, w_send, w_recv):
     tm = lax.axis_index("tm")
     me = lax.axis_index("chan")
     n_rows, n_cols = record.shape
@@ -217,23 +218,39 @@
             crossp[level, 0:r] = dot3(split(stk[level, got_rows]), own, NT)
             half = pl.ds(pl.multiple_of(core * h, 8), h)
             away = pl.ds(pl.multiple_of((1 - core) * h, 8), h)
-            pre_copy = remote(crossp.at[level, away], pre.at[level, pl.ds(0, h)], pre_sem.at[0, level], pre_sem.at[1, level],
-                              {"chan": other_core})
+            direct = h == 8
+            if direct:
+                peers = []
+                for o in offsets:
+                    peer = lax.rem(me + o, n_chan)
+                    rows_there = pl.ds(pl.multiple_of(lax.rem(peer, 2) * h, 8), h)
+                    peers.append(remote(crossp.at[level, rows_there], wide.at[level, me],
+                                        w_send.at[level, o], w_recv.at[level, o], {"chan": peer}))
+                wide[level, me] = crossp[level, half]
+            else:
+                pre_copy = remote(crossp.at[level, away], pre.at[level, pl.ds(0, h)],
+                                  pre_sem.at[0, level], pre_sem.at[1, level], {"chan": other_core})
             forwards = []
             for i in range(1, count):
                 forwards.append(remote(stk.at[level, got_rows], stk.at[level, got_rows],
                                        f_send.at[level, i], f_recv.at[level, i], {"tm": member(count, i)}))
-            pre_copy.wait()
-            slot = zbuf.at[level, z_me, pl.ds(0, h)]
-            slot[...] = crossp[level, half] + pre[level, 0:h]
-            copies = []
-            for o in z_offsets:
-                peer = lax.rem(me + 2 * o, n_chan)
-                copies.append(remote(slot, slot, z_send.at[level, o], z_recv.at[level, o], {"chan": peer}))
-            for copy in copies:
-                copy.wait()
+            if direct:
+                for copy in peers:
+                    copy.wait()
+                total = jnp.sum(wide[level], axis=0)
+            else:
+                pre_copy.wait()
+                slot = zbuf.at[level, z_me, pl.ds(0, h)]
+                slot[...] = crossp[level, half] + pre[level, 0:h]
+                copies = []
+                for o in z_offsets:
+                    peer = lax.rem(me + 2 * o, n_chan)
+                    copies.append(remote(slot, slot, z_send.at[level, o], z_recv.at[level, o], {"chan": peer}))
+                for copy in copies:
+                    copy.wait()
+                total = jnp.sum(zbuf[level, :, 0:h], axis=0)
             chunk = cross.at[level, pl.ds(pl.multiple_of(place * r + core * h, 8), h)]
-            chunk[...] = jnp.sum(zbuf[level, :, 0:h], axis=0)
+            chunk[...] = total
             copies = []
             for i in range(count - 1, -1, -1):
                 for d in range(2):
@@ -258,6 +275,10 @@
         shifted = value - mean * eye
         z = shifted / jnp.sqrt(jnp.sum(shifted * shifted, keepdims=True) + 1e-06)
         for step in range(K_ITERS):
+            if step < COARSE:
+                rounded = z.astype(BF16)
+                z = 1.5 * z - 0.5 * dot(rounded, dot(rounded, rounded).astype(BF16))
+                continue
             parts = split(z)
             z = 1.5 * z - 0.5 * dot3(parts, split(dot3(parts, parts)))
 
@@ -324,6 +345,7 @@
             pltpu.VMEM((levels, RANK // 2, RANK), F32),
             pltpu.VMEM((levels, RANK // 4, RANK), F32),
             pltpu.VMEM((levels, n_chan // 2, RANK // 4, RANK), F32),
+            pltpu.VMEM((levels, n_chan, 8, RANK), F32),
             pltpu.VMEM((levels, RANK, RANK), F32),
             pltpu.VMEM((levels, RANK // 2, n_cols), F32),
             pltpu.VMEM((RANK, 2 * RANK), BF16),
@@ -343,6 +365,8 @@
             dma((levels, 2 * most)),
             dma((levels, most)),
             dma((levels, most)),
+            dma((levels, n_chan)),
+            dma((levels, n_chan)),
         ],
         compiler_params=pltpu.CompilerParams(collective_id=0, has_side_effects=True, vmem_limit_bytes=67_000_000),
     )(record, fir_taps, gauge_lag, projector, compress)

time: 140 us -> 134 us (0.957)
  Pallas kernels: 138 us -> 133 us
    pallas_call x1, Pallas kernels: 138 us -> 133 us  [on_device(): pl.pallas_call(functools.partial(kernel, n_tm, n_chan, levels), out_shape...]
where the time goes in v4:
time: 134 us
  Pallas kernels  133 us (99%)
    pallas_call x1, Pallas kernels, on_device(): pl.pallas_call(functools.partial(kernel, n_tm, n_chan, levels), out_shape...  133 us

profile of v4, /device:TPU:1, one launch (start us, length us, event | category | flops | bytes accessed | tf_op | source)
XLA Modules:
  0.0 134.3 jit_solution(5857422223254413216)
XLA Ops:
  0.0 133.0 %shard_map.55 = f32[4,640]{1,0:T(4,128)} custom-call(bf16[1024,640]{1,0:T(8,128)(2,1)} %record.1, bf16[64]{0:T(256)(128)(2,1)} %taps_hbm.1, s32[640]{0:T(1024)} %lag_hbm.1, bf16[1024,128]{1,0:T(8,128)(2,1)} %proj_hbm.1, f32[256,128]{1,0:T(8,128)} %comp_hbm.1), custom_call_target="tpu_custom_call" | custom-call | tf_op jit(solution)/shard_map/pallas_call | solution.py:323
  133.0 1.3 copy.7

commit v5 on v4

--- a/solution.py
+++ b/solution.py
@@ -14,7 +14,7 @@
 RANK = 128
 BLOCK = 128
 MOST = 8
-COARSE = 5
+COARSE = 7
 MESH = pl.DeviceIdType.MESH
 F32 = jnp.float32
 BF16 = jnp.bfloat16
@@ -41,7 +41,7 @@
 
 def kernel(n_tm, n_chan, levels, record, taps_hbm, lag_hbm, proj_hbm, comp_hbm, out_ref,
            ext, filtered, strain, proj_ref, comp_ref, taps_ref, lag_ref, stk, stk_hi, stk_lo, gram, diag, comp_t, part, scat, gath,
-           crossp, pre, zbuf, wide, cross, ahead, mix_hi, mix_lo,
+           crossp, pre, zbuf, wide, cross, ahead_hi, ahead_lo, mix_hi, mix_lo,
            local_sem, halo_sem, ex_sem, dg_sem, rs_send, rs_recv, ag_send, ag_recv,
            pre_sem, z_send, z_recv, g_send, g_recv, f_send, f_recv, w_send, w_recv):
     tm = lax.axis_index("tm")
@@ -130,7 +130,7 @@
     halo.start()
     load_proj.wait()
     late = 2 * BLOCK
-    stk[0, 0:RANK] = dot(proj_ref[late:], strain[late:], TN)
+    stk[0] = dot(proj_ref[late:], strain[late:], TN)
     load_comp.wait()
     comp = comp_ref[...].T
     comp_t[0] = comp
@@ -145,7 +145,7 @@
     def _(block):
         difference(block)
 
-    stk[0, 0:RANK] += dot(proj_ref[0:late], strain[0:late], TN)
+    stk[0] += dot(proj_ref[0:late], strain[0:late], TN)
 
     def remote(src, dst, send_sem, recv_sem, who):
         copy = pltpu.make_async_remote_copy(
@@ -184,11 +184,19 @@
     eye = (lax.broadcasted_iota(jnp.int32, (2 * RANK, 2 * RANK), 0)
            == lax.broadcasted_iota(jnp.int32, (2 * RANK, 2 * RANK), 1)).astype(F32)
 
-    def split_rows(level, low, count):
-        high, rest = split(stk[level, low:low + count])
-        stk_hi[low:low + count] = high
-        stk_lo[low:low + count] = rest
+    def split_rows(level):
+        high, rest = split(stk[level])
+        stk_hi[level, 0:RANK] = high
+        stk_lo[level, 0:RANK] = rest
         return high, rest
+
+    def send_rows(level, high, rest, where):
+        who = {"tm": partners[level]}
+        return (remote(high, stk_hi.at[level, where], ex_sem.at[0, level], ex_sem.at[1, level], who),
+                remote(rest, stk_lo.at[level, where], ex_sem.at[2, level], ex_sem.at[3, level], who))
+
+    def cross_rows(received, own):
+        return dot(received, own[0], NT) + dot(received, own[1], NT)
 
     for level in range(levels):
         count = min(2**level, most)
@@ -196,16 +204,17 @@
         h = r // 2
         last = level == levels - 1
         place = lax.rem(tm, count)
-        got_rows = pl.ds(pl.multiple_of(RANK + place * r, 8), r)
+        got_rows = pl.ds(pl.multiple_of(RANK + place * r, 16), r)
+        own = split_rows(level)
         if level == 0:
-            moving = remote(stk.at[0, pl.ds(0, RANK)], stk.at[0, pl.ds(RANK, RANK)], ex_sem.at[0, 0], ex_sem.at[1, 0],
-                            {"tm": partners[0]})
-        own = split_rows(level, 0, RANK)
+            upper_half = pl.ds(RANK, RANK)
+            moving, moving_low = send_rows(0, stk_hi.at[0, pl.ds(0, RANK)], stk_lo.at[0, pl.ds(0, RANK)], upper_half)
         if level == 0:
             diag_moving = scatter(0, dot3(own, own, NT))
             diag_moving = gather(0, diag_moving)
             moving.wait()
-            cross_moving = scatter(1, dot3(split_rows(0, RANK, RANK), own, NT))
+            cross_moving = scatter(1, cross_rows(stk_hi[0, RANK:], own))
+            moving_low.wait()
             diag[0, 0] = finish(0, diag_moving)
             diag_copy = send_diag(0)
             cross_moving = gather(1, cross_moving)
@@ -215,7 +224,7 @@
             diag[level, 0] = dot3(split(dot3(mix, split(gram[...]))), mix, NT)
             diag_copy = send_diag(level)
             moving.wait()
-            crossp[level, 0:r] = dot3(split(stk[level, got_rows]), own, NT)
+            crossp[level, 0:r] = cross_rows(stk_hi[level, got_rows], own)
             half = pl.ds(pl.multiple_of(core * h, 8), h)
             away = pl.ds(pl.multiple_of((1 - core) * h, 8), h)
             direct = h == 8
@@ -231,9 +240,12 @@
                 pre_copy = remote(crossp.at[level, away], pre.at[level, pl.ds(0, h)],
                                   pre_sem.at[0, level], pre_sem.at[1, level], {"chan": other_core})
             forwards = []
+            moving_low.wait()
             for i in range(1, count):
-                forwards.append(remote(stk.at[level, got_rows], stk.at[level, got_rows],
-                                       f_send.at[level, i], f_recv.at[level, i], {"tm": member(count, i)}))
+                for k, side in enumerate((stk_hi, stk_lo)):
+                    forwards.append(remote(side.at[level, got_rows], side.at[level, got_rows],
+                                           f_send.at[level, 2 * i + k], f_recv.at[level, 2 * i + k],
+                                           {"tm": member(count, i)}))
             if direct:
                 for copy in peers:
                     copy.wait()
@@ -259,7 +271,6 @@
                         copies.append(remote(chunk, chunk, g_send.at[level, 2 * i + d], g_recv.at[level, 2 * i + d], who))
             for copy in forwards:
                 copy.wait()
-            split_rows(level, RANK, RANK)
             for copy in copies:
                 copy.wait()
             below = cross[level]
@@ -284,7 +295,7 @@
 
         upper = lax.rem(tm // 2**level, 2)
         parts = split(z)
-        both = (stk_hi[...], stk_lo[...])
+        both = (stk_hi[level], stk_lo[level])
 
         def mixed(rows):
             mine = comp_t[upper, rows]
@@ -294,13 +305,15 @@
             after = min(2 * 2**level, most)
             size = RANK // after
             spot = lax.rem(tm, after) * size
-            ahead[level + 1, 0:size] = dot3(mixed(pl.ds(pl.multiple_of(spot, 8), size)), both)
-            moving = remote(ahead.at[level + 1, pl.ds(0, size)],
-                            stk.at[level + 1, pl.ds(pl.multiple_of(RANK + spot, 8), size)],
-                            ex_sem.at[0, level + 1], ex_sem.at[1, level + 1], {"tm": partners[level + 1]})
+            early, early_low = split(dot3(mixed(pl.ds(pl.multiple_of(spot, 16), size)), both))
+            ahead_hi[level + 1, 0:size] = early
+            ahead_lo[level + 1, 0:size] = early_low
+            moving, moving_low = send_rows(level + 1, ahead_hi.at[level + 1, pl.ds(0, size)],
+                                           ahead_lo.at[level + 1, pl.ds(0, size)],
+                                           pl.ds(pl.multiple_of(RANK + spot, 16), size))
             mix = mixed(pl.ds(0, RANK))
             mix_hi[...], mix_lo[...] = mix
-            stk[level + 1, 0:RANK] = dot3(mix, both)
+            stk[level + 1] = dot3(mix, both)
         else:
             share = RANK // n_tm
             group = max(8, share)
@@ -333,9 +346,9 @@
             pltpu.VMEM((2 * RANK, RANK), F32),
             pltpu.VMEM((TAPS,), BF16),
             pltpu.VMEM((n_cols,), jnp.int32),
-            pltpu.VMEM((levels, 2 * RANK, n_cols), F32),
-            pltpu.VMEM((2 * RANK, n_cols), BF16),
-            pltpu.VMEM((2 * RANK, n_cols), BF16),
+            pltpu.VMEM((levels, RANK, n_cols), F32),
+            pltpu.VMEM((levels, 2 * RANK, n_cols), BF16),
+            pltpu.VMEM((levels, 2 * RANK, n_cols), BF16),
             pltpu.VMEM((2 * RANK, 2 * RANK), F32),
             pltpu.VMEM((levels, 2, RANK, RANK), F32),
             pltpu.VMEM((2, RANK, 2 * RANK), F32),
@@ -347,12 +360,13 @@
             pltpu.VMEM((levels, n_chan // 2, RANK // 4, RANK), F32),
             pltpu.VMEM((levels, n_chan, 8, RANK), F32),
             pltpu.VMEM((levels, RANK, RANK), F32),
-            pltpu.VMEM((levels, RANK // 2, n_cols), F32),
+            pltpu.VMEM((levels, RANK // 2, n_cols), BF16),
+            pltpu.VMEM((levels, RANK // 2, n_cols), BF16),
             pltpu.VMEM((RANK, 2 * RANK), BF16),
             pltpu.VMEM((RANK, 2 * RANK), BF16),
             dma((5,)),
             dma((2,)),
-            dma((2, levels)),
+            dma((4, levels)),
             dma((2, levels)),
             dma((2, n_chan)),
             dma((2, n_chan)),
@@ -363,8 +377,8 @@
             dma((levels, n_chan // 2)),
             dma((levels, 2 * most)),
             dma((levels, 2 * most)),
-            dma((levels, most)),
-            dma((levels, most)),
+            dma((levels, 2 * most)),
+            dma((levels, 2 * most)),
             dma((levels, n_chan)),
             dma((levels, n_chan)),
         ],

time: 134 us -> 123 us (0.918); the launches traced: 134 us -> 122 us
  Pallas kernels: 133 us -> 120 us
    pallas_call x1, Pallas kernels: 133 us -> 120 us  [on_device(): pl.pallas_call(functools.partial(kernel, n_tm, n_chan, levels), out_shape...]
where the time goes in v5:
time: 123 us; the launch traced here: 122 us
  Pallas kernels  120 us (98%)
  local copies, waits for them, and re-layouts  1.3 us (1%)
    pallas_call x1, Pallas kernels, on_device(): pl.pallas_call(functools.partial(kernel, n_tm, n_chan, levels), out_shape...  120 us

profile of v5, /device:TPU:1, one launch (start us, length us, event | category | flops | bytes accessed | tf_op | source)
XLA Modules:
  0.0 121.5 jit_solution(12609937098854976926)
XLA Ops:
  0.0 120.2 %shard_map.55 = f32[4,640]{1,0:T(4,128)} custom-call(bf16[1024,640]{1,0:T(8,128)(2,1)} %record.1, bf16[64]{0:T(256)(128)(2,1)} %taps_hbm.1, s32[640]{0:T(1024)} %lag_hbm.1, bf16[1024,128]{1,0:T(8,128)(2,1)} %proj_hbm.1, f32[256,128]{1,0:T(8,128)} %comp_hbm.1), custom_call_target="tpu_custom_call" | custom-call | tf_op jit(solution)/shard_map/pallas_call | solution.py:336
  120.2 1.3 %copy.7 = f32[4,640]{1,0:T(4,128)} copy(f32[4,640]{1,0:T(4,128)} %shard_map.55) | data formatting | bytes 20480

commit v6 on v5

--- a/solution.py
+++ b/solution.py
@@ -41,7 +41,7 @@
 
 def kernel(n_tm, n_chan, levels, record, taps_hbm, lag_hbm, proj_hbm, comp_hbm, out_ref,
            ext, filtered, strain, proj_ref, comp_ref, taps_ref, lag_ref, stk, stk_hi, stk_lo, gram, diag, comp_t, part, scat, gath,
-           crossp, pre, zbuf, wide, cross, ahead_hi, ahead_lo, mix_hi, mix_lo,
+           crossp, crossp_b, pre, zbuf, wide, cross, cross_b, ahead_hi, ahead_lo, mix_hi, mix_lo,
            local_sem, halo_sem, ex_sem, dg_sem, rs_send, rs_recv, ag_send, ag_recv,
            pre_sem, z_send, z_recv, g_send, g_recv, f_send, f_recv, w_send, w_recv):
     tm = lax.axis_index("tm")
@@ -224,10 +224,14 @@
             diag[level, 0] = dot3(split(dot3(mix, split(gram[...]))), mix, NT)
             diag_copy = send_diag(level)
             moving.wait()
-            crossp[level, 0:r] = cross_rows(stk_hi[level, got_rows], own)
-            half = pl.ds(pl.multiple_of(core * h, 8), h)
-            away = pl.ds(pl.multiple_of((1 - core) * h, 8), h)
             direct = h == 8
+            align = min(h, 16)
+            value = cross_rows(stk_hi[level, got_rows], own)
+            crossp[level, 0:r] = value
+            if not direct:
+                crossp_b[level, 0:r] = value.astype(BF16)
+            half = pl.ds(pl.multiple_of(core * h, align), h)
+            away = pl.ds(pl.multiple_of((1 - core) * h, align), h)
             if direct:
                 peers = []
                 for o in offsets:
@@ -237,7 +241,7 @@
                                         w_send.at[level, o], w_recv.at[level, o], {"chan": peer}))
                 wide[level, me] = crossp[level, half]
             else:
-                pre_copy = remote(crossp.at[level, away], pre.at[level, pl.ds(0, h)],
+                pre_copy = remote(crossp_b.at[level, away], pre.at[level, pl.ds(0, h)],
                                   pre_sem.at[0, level], pre_sem.at[1, level], {"chan": other_core})
             forwards = []
             moving_low.wait()
@@ -253,16 +257,17 @@
             else:
                 pre_copy.wait()
                 slot = zbuf.at[level, z_me, pl.ds(0, h)]
-                slot[...] = crossp[level, half] + pre[level, 0:h]
+                slot[...] = (crossp[level, half] + pre[level, 0:h].astype(F32)).astype(BF16)
                 copies = []
                 for o in z_offsets:
                     peer = lax.rem(me + 2 * o, n_chan)
                     copies.append(remote(slot, slot, z_send.at[level, o], z_recv.at[level, o], {"chan": peer}))
                 for copy in copies:
                     copy.wait()
-                total = jnp.sum(zbuf[level, :, 0:h], axis=0)
-            chunk = cross.at[level, pl.ds(pl.multiple_of(place * r + core * h, 8), h)]
-            chunk[...] = total
+                total = jnp.sum(zbuf[level, :, 0:h].astype(F32), axis=0)
+            joined = cross if direct else cross_b
+            chunk = joined.at[level, pl.ds(pl.multiple_of(place * r + core * h, align), h)]
+            chunk[...] = total.astype(chunk.dtype)
             copies = []
             for i in range(count - 1, -1, -1):
                 for d in range(2):
@@ -273,7 +278,7 @@
                 copy.wait()
             for copy in copies:
                 copy.wait()
-            below = cross[level]
+            below = joined[level].astype(F32)
 
         gram[RANK:, 0:RANK] = below
         gram[0:RANK, RANK:] = below.T
@@ -356,10 +361,12 @@
             pltpu.VMEM((2, n_chan, slice_rows, RANK), F32),
             pltpu.VMEM((2, n_chan, slice_rows, RANK), F32),
             pltpu.VMEM((levels, RANK // 2, RANK), F32),
-            pltpu.VMEM((levels, RANK // 4, RANK), F32),
-            pltpu.VMEM((levels, n_chan // 2, RANK // 4, RANK), F32),
+            pltpu.VMEM((levels, RANK // 2, RANK), BF16),
+            pltpu.VMEM((levels, RANK // 4, RANK), BF16),
+            pltpu.VMEM((levels, n_chan // 2, RANK // 4, RANK), BF16),
             pltpu.VMEM((levels, n_chan, 8, RANK), F32),
             pltpu.VMEM((levels, RANK, RANK), F32),
+            pltpu.VMEM((levels, RANK, RANK), BF16),
             pltpu.VMEM((levels, RANK // 2, n_cols), BF16),
             pltpu.VMEM((levels, RANK // 2, n_cols), BF16),
             pltpu.VMEM((RANK, 2 * RANK), BF16),

time: 123 us -> 123 us (level)
  no operation moved by 1% of the time
where the time goes in v6:
time: 123 us
  Pallas kernels  121 us (98%)
  local copies, waits for them, and re-layouts  1.3 us (1%)
    pallas_call x1, Pallas kernels, on_device(): pl.pallas_call(functools.partial(kernel, n_tm, n_chan, levels), out_shape...  121 us

profile of v6, /device:TPU:1, one launch (start us, length us, event | category | flops | bytes accessed | tf_op | source)
XLA Modules:
  0.0 122.7 jit_solution(11218810012829130382)
XLA Ops:
  0.0 121.4 %shard_map.55 = f32[4,640]{1,0:T(4,128)} custom-call(bf16[1024,640]{1,0:T(8,128)(2,1)} %record.1, bf16[64]{0:T(256)(128)(2,1)} %taps_hbm.1, s32[640]{0:T(1024)} %lag_hbm.1, bf16[1024,128]{1,0:T(8,128)(2,1)} %proj_hbm.1, f32[256,128]{1,0:T(8,128)} %comp_hbm.1), custom_call_target="tpu_custom_call" | custom-call | tf_op jit(solution)/shard_map/pallas_call | solution.py:341
  121.4 1.3 %copy.7 = f32[4,640]{1,0:T(4,128)} copy(f32[4,640]{1,0:T(4,128)} %shard_map.55) | data formatting | bytes 20480

commit v7 on v6

--- a/solution.py
+++ b/solution.py
@@ -244,13 +244,16 @@
                 pre_copy = remote(crossp_b.at[level, away], pre.at[level, pl.ds(0, h)],
                                   pre_sem.at[0, level], pre_sem.at[1, level], {"chan": other_core})
             forwards = []
-            moving_low.wait()
-            for i in range(1, count):
-                for k, side in enumerate((stk_hi, stk_lo)):
-                    forwards.append(remote(side.at[level, got_rows], side.at[level, got_rows],
-                                           f_send.at[level, 2 * i + k], f_recv.at[level, 2 * i + k],
-                                           {"tm": member(count, i)}))
+            def pass_on():
+                moving_low.wait()
+                for i in range(1, count):
+                    for k, side in enumerate((stk_hi, stk_lo)):
+                        forwards.append(remote(side.at[level, got_rows], side.at[level, got_rows],
+                                               f_send.at[level, 2 * i + k], f_recv.at[level, 2 * i + k],
+                                               {"tm": member(count, i)}))
+
             if direct:
+                pass_on()
                 for copy in peers:
                     copy.wait()
                 total = jnp.sum(wide[level], axis=0)
@@ -262,6 +265,7 @@
                 for o in z_offsets:
                     peer = lax.rem(me + 2 * o, n_chan)
                     copies.append(remote(slot, slot, z_send.at[level, o], z_recv.at[level, o], {"chan": peer}))
+                pass_on()
                 for copy in copies:
                     copy.wait()
                 total = jnp.sum(zbuf[level, :, 0:h].astype(F32), axis=0)

time: 123 us -> 121 us (0.984)
  Pallas kernels: 121 us -> 119 us
    pallas_call x1, Pallas kernels: 121 us -> 119 us  [on_device(): pl.pallas_call(functools.partial(kernel, n_tm, n_chan, levels), out_shape...]
where the time goes in v7:
time: 121 us; the launch traced here: 120 us
  Pallas kernels  119 us (98%)
  local copies, waits for them, and re-layouts  1.3 us (1%)
    pallas_call x1, Pallas kernels, on_device(): pl.pallas_call(functools.partial(kernel, n_tm, n_chan, levels), out_shape...  119 us

profile of v7, /device:TPU:1, one launch (start us, length us, event | category | flops | bytes accessed | tf_op | source)
XLA Modules:
  0.0 119.9 jit_solution(7044236830490438873)
XLA Ops:
  0.0 118.6 %shard_map.55 = f32[4,640]{1,0:T(4,128)} custom-call(bf16[1024,640]{1,0:T(8,128)(2,1)} %record.1, bf16[64]{0:T(256)(128)(2,1)} %taps_hbm.1, s32[640]{0:T(1024)} %lag_hbm.1, bf16[1024,128]{1,0:T(8,128)(2,1)} %proj_hbm.1, f32[256,128]{1,0:T(8,128)} %comp_hbm.1), custom_call_target="tpu_custom_call" | custom-call | tf_op jit(solution)/shard_map/pallas_call | solution.py:345
  118.6 1.3 %copy.7 = f32[4,640]{1,0:T(4,128)} copy(f32[4,640]{1,0:T(4,128)} %shard_map.55) | data formatting | bytes 20480
